TPU v7x, 256 devices: a whole 4x4x8 slice. The times are simulated.
256 devices in a mesh: img: 16 (over z, core), txt: 16 (over x, y).
Axes of the slice: x: 4, y: 4, z: 8, core: 2. Of those that a mesh axis runs over, the one named last changes fastest.
Arguments:
- teacher_img: bfloat16 [16384, 1280], P('img'), may hold values from -40 to 40
- teacher_txt: bfloat16 [16384, 1280], P('txt'), may hold values from -40 to 40
- student_img: bfloat16 [16384, 512], P('img'), may hold values from -40 to 40
- student_txt: bfloat16 [16384, 512], P('txt'), may hold values from -40 to 40
Outputs:
- loss: float32 [], replicated
- grad_img: float32 [16384, 512], P(('img', 'txt'))
- grad_txt: float32 [16384, 512], P(('txt', 'img'))
All inputs are finite; a program needn't handle non-finite values.
Results may differ from a plain program's by a relative error of at most 0.0033.
Values sent between devices are 32-bit elements; how exact they have to be, the bound alone decides.
No kernel may reach another device: no remote copies, remote signals or barrier semaphores. Data moves between devices by JAX's collectives and lax.ppermute only.
A program may use at most 64 MiB of HBM per device.

v0:
```python
import math
import jax
import jax.numpy as jnp
from jax import lax
from jax.sharding import Mesh
from jax.sharding import PartitionSpec as P

IMG = ("img_0", "img_1")
TXT = ("txt_0", "txt_1")
IMG_TXT = ("img_0", "img_1", "txt_0", "txt_1")
TXT_IMG = ("txt_0", "txt_1", "img_0", "img_1")


def from_everyone(shard, axis):
    copies = jnp.broadcast_to(shard, (lax.axis_size(axis), *shard.shape))
    return lax.all_to_all(copies, axis, split_axis=0, concat_axis=0, tiled=True)


def collected_together(shard, axis):
    leaves = jax.tree.leaves(shard)
    order = sorted(range(len(leaves)), key=lambda k: -leaves[k].size)
    width = (1, *leaves[order[0]].shape)[-1]
    lines = [
        jnp.pad(leaves[k].reshape(-1), (0, -leaves[k].size % width)).reshape(-1, width)
        for k in order
    ]
    both, at, found = (from_everyone(jnp.concatenate(lines), axis), 0, {})
    for k, line in zip(order, lines):
        piece = both[:, at : at + len(line)].reshape(len(both), -1)
        found[k] = piece[:, : leaves[k].size].reshape(-1, *leaves[k].shape)
        at += len(line)
    numbers = iter(range(len(leaves)))
    return jax.tree.map(lambda _: found[next(numbers)], shard)


def combined_pairwise(pieces, combine):
    while len(jax.tree.leaves(pieces)[0]) > 1:
        pieces = jax.vmap(combine)(
            *(jax.tree.map(lambda part: part[side::2], pieces) for side in (0, 1))
        )
    return jax.tree.map(lambda part: part[0], pieces)


def joined_all(shard, axis, combine):
    pieces = collected_together(shard, axis)
    return combined_pairwise(pieces, combine)


def over_axes(shard, axes):
    for axis in axes:
        shard = lax.psum(shard, axis)
    return shard


def split_up(shard, dim, size):
    dims = shard.shape
    parts = shard.reshape(*dims[:dim], size, dims[dim] // size, *dims[dim + 1 :])
    return jnp.moveaxis(parts, dim, 0)


def sum_by_chip(shard, chips, core, dim):
    sizes = (lax.axis_size(chips), lax.axis_size(core))
    parts = split_up(shard, dim, sizes[0] * sizes[1])
    inside = parts.shape[1:]
    parts = parts.reshape(*sizes, *inside).swapaxes(0, 1).reshape(-1, *inside)
    parts = lax.psum_scatter(parts, core, scatter_dimension=0, tiled=True)
    return lax.psum_scatter(parts, chips, scatter_dimension=0, tiled=True)[0]


def summed_on_arrival(shard, axis, dim):
    size = lax.axis_size(axis)
    parts = lax.all_to_all(split_up(shard, dim, size), axis, 0, 0, tiled=True)
    return jnp.sum(parts, axis=0)


def join_pair(peak_one, mass_one, peak_two, mass_two):
    highest = jnp.maximum(peak_one, peak_two)
    return (
        highest,
        mass_one * jnp.exp(peak_one - highest) + mass_two * jnp.exp(peak_two - highest),
    )


def combine_masses(first, second):
    teach_peak, teach_mass = join_pair(first[0], first[1], second[0], second[1])
    learn_peak, learn_mass = join_pair(first[2], first[3], second[2], second[3])
    return (teach_peak, teach_mass, learn_peak, learn_mass)


def local_masses(teacher, student, along):
    teach_peak = jnp.max(teacher, axis=along)
    learn_peak = jnp.max(student, axis=along)
    teach_mass = jnp.sum(jnp.exp(teacher - jnp.expand_dims(teach_peak, along)), axis=along)
    learn_mass = jnp.sum(jnp.exp(student - jnp.expand_dims(learn_peak, along)), axis=along)
    return (teach_peak, teach_mass, learn_peak, learn_mass)


def body(teacher_img, teacher_txt, student_img, student_txt):
    scale_teach = 3.0 / math.sqrt(teacher_img.shape[1])
    scale_learn = 3.0 / math.sqrt(student_img.shape[1])
    rows = teacher_img.shape[0]
    cols = teacher_txt.shape[0]
    img_count = lax.axis_size(IMG)
    txt_count = lax.axis_size(TXT)
    teacher = scale_teach * jnp.einsum(
        "id,jd->ij", teacher_img, teacher_txt, preferred_element_type=jnp.float32
    )
    student = scale_learn * jnp.einsum(
        "id,jd->ij", student_img, student_txt, preferred_element_type=jnp.float32
    )
    row_tpeak, row_tmass, row_lpeak, row_lmass = joined_all(
        local_masses(teacher, student, 1), TXT, combine_masses
    )
    col_tpeak, col_tmass, col_lpeak, col_lmass = joined_all(
        local_masses(teacher, student, 0), IMG, combine_masses
    )
    row_teach = row_tpeak + jnp.log(row_tmass)
    row_learn = row_lpeak + jnp.log(row_lmass)
    col_teach = col_tpeak + jnp.log(col_tmass)
    col_learn = col_lpeak + jnp.log(col_lmass)
    p_row = jnp.exp(teacher - row_teach[:, None])
    q_row = jnp.exp(student - row_learn[:, None])
    p_col = jnp.exp(teacher - col_teach[None, :])
    q_col = jnp.exp(student - col_learn[None, :])
    gap = teacher - student
    row_part = (jnp.sum(p_row * gap) + jnp.sum(row_learn - row_teach) / txt_count) / (
        rows * img_count
    )
    col_part = (jnp.sum(p_col * gap) + jnp.sum(col_learn - col_teach) / img_count) / (
        cols * txt_count
    )
    delta = (8.0 * (q_row - p_row + q_col - p_col)).astype(jnp.bfloat16)
    loss = 0.5 * over_axes(row_part + col_part, IMG_TXT)
    picked = delta
    grad_txt = sum_by_chip(
        scale_learn
        * jnp.einsum("ij,id->jd", picked, student_img, preferred_element_type=jnp.float32),
        "img_0",
        "img_1",
        0,
    )
    picked = delta
    grad_img = summed_on_arrival(
        scale_learn * jnp.dot(picked, student_txt, preferred_element_type=jnp.float32), TXT, 0
    )
    return (loss, grad_img, grad_txt)


def solution(mesh):
    torus = Mesh(mesh.devices.reshape(8, 2, 4, 4), ("img_0", "img_1", "txt_0", "txt_1"))
    in_specs = (P(IMG, None), P(TXT, None), P(IMG, None), P(TXT, None))
    out_specs = (P(), P(IMG_TXT, None), P(TXT_IMG, None))
    return jax.shard_map(body, mesh=torus, in_specs=in_specs, out_specs=out_specs, check_vma=False)
```

profile of v0, /device:TPU:0, one launch (start us, length us, event | category | flops | bytes accessed | tf_op | source)
XLA Modules:
  0.0 146.1 jit_solution(15397041045933169511)
XLA Ops:
  7.2 0.0 copy-start
  7.2 0.0 copy-start.4
  7.2 1.7 %copy-done = bf16[1024,1280]{1,0:T(8,128)(2,1)S(1)} copy-done((bf16[1024,1280]{1,0:T(8,128)(2,1)S(1)}, bf16[1024,1280]{1,0:T(8,128)(2,1)}, u32[]{:S(2)}) %copy-start) | copy-done | bytes 2621464
  8.9 0.0 copy-start.6
  8.9 4.8 %multiply_reduce_fusion.4 = (f32[1024]{0:T(1024)S(1)}, f32[1024]{0:T(1024)S(1)}, f32[1024,1024]{1,0:T(8,128)S(1)}) fusion(bf16[1024,1280]{1,0:T(8,128)(2,1)S(1)} %copy-done, bf16[1024,1280]{1,0:T(8,128)(2,1)} %param.5), kind=kOutput, calls=%fused_computation.12 | convolution fusion | flops 2687498240 | bytes 9445376 | tf_op jit(solution)/shard_map/id,jd->ij/dot_general | solution.py:105
  13.7 0.0 copy-done.4
  13.7 0.0 copy-done.6
  13.7 0.0 copy-start.1
  13.7 1.4 multiply_reduce_fusion.2
  15.1 0.0 copy-start.2
  15.1 0.6 copy-done.1
  15.7 1.6 %exponential_reduce_fusion.1 = (f32[1024]{0:T(1024)S(1)}, f32[1024]{0:T(1024)S(1)}) fusion(f32[1024,1024]{1,0:T(8,128)S(1)} %get-tuple-element.50, f32[1024]{0:T(1024)S(1)} %get-tuple-element.7, f32[1024]{0:T(1024)S(1)} %get-tuple-element.8), kind=kLoop, calls=%fused_computation.4 | loop fusion | flops 5240832 | bytes 4210688 | tf_op jit(solution)/shard_map/reduce_sum | solution.py:93
  17.3 1.6 %exponential_reduce_fusion = (f32[1024]{0:T(1024)S(1)}, f32[1024]{0:T(1024)S(1)}) fusion(f32[1024,1024]{1,0:T(8,128)S(1)} %get-tuple-element.49, f32[1024]{0:T(1024)S(1)} %get-tuple-element.11, f32[1024]{0:T(1024)S(1)} %get-tuple-element.12), kind=kLoop, calls=%fused_computation.3 | loop fusion | flops 5240832 | bytes 4210688 | tf_op jit(solution)/shard_map/reduce_sum | solution.py:94
  18.8 0.0 copy-done.2
  18.9 0.8 broadcast_in_dim.4
  19.6 5.3 %all-to-all-start = ((f32[16,4,1024]{2,1,0:T(4,128)}), f32[16,4,1024]{2,1,0:T(4,128)S(1)}, u32[]{:S(2)}, u32[]{:S(2)}) async-start(f32[16,4,1024]{2,1,0:T(4,128)} %broadcast_in_dim.4), calls=%async_computation | async-start | bytes 524288 | tf_op jit(solution)/shard_map/all_to_all | solution.py:16
  25.0 8.5 %all-to-all-done = f32[16,4,1024]{2,1,0:T(4,128)S(1)} async-done(((f32[16,4,1024]{2,1,0:T(4,128)}), f32[16,4,1024]{2,1,0:T(4,128)S(1)}, u32[]{:S(2)}, u32[]{:S(2)}) %all-to-all-start) | async-done | bytes 262176 | tf_op jit(solution)/shard_map/all_to_all | solution.py:16
  33.4 0.8 broadcast_in_dim.5
  34.2 8.6 %all-to-all-start.1 = ((f32[16,4,1024]{2,1,0:T(4,128)}), f32[16,4,1024]{2,1,0:T(4,128)S(1)}, u32[]{:S(2)}, u32[]{:S(2)}) async-start(f32[16,4,1024]{2,1,0:T(4,128)} %broadcast_in_dim.5), calls=%async_computation.1 | async-start | bytes 524288 | tf_op jit(solution)/shard_map/all_to_all | solution.py:16
  42.8 0.2 reduce-scatter.3.cloned.1.call-start
  43.0 0.2 fusion.8
  44.1 9.9 %all-to-all-done.1 = f32[16,4,1024]{2,1,0:T(4,128)S(1)} async-done(((f32[16,4,1024]{2,1,0:T(4,128)}), f32[16,4,1024]{2,1,0:T(4,128)S(1)}, u32[]{:S(2)}, u32[]{:S(2)}) %all-to-all-start.1) | async-done | bytes 262176 | tf_op jit(solution)/shard_map/all_to_all | solution.py:16
  54.0 0.2 fusion.9
  55.0 0.7 subtract_reduce_fusion
  55.6 0.0 copy-start.5
  55.6 9.1 %multiply_reduce_fusion = (f32[]{:T(128)}, f32[]{:T(128)}, bf16[1024,1024]{1,0:T(8,128)(2,1)S(1)}) fusion(f32[1024,1024]{1,0:T(8,128)} %copy-done.2, f32[1024,1024]{1,0:T(8,128)} %copy-done.1, f32[1024]{0:T(1024)S(1)} %bitcast.50, f32[1024]{0:T(1024)S(1)} %bitcast.47, f32[1024]{0:T(1024)S(1)} %bitcast.49, f32[1024]{0:T(1024)S(1)} %bitcast.45), kind=kLoop, calls=%fused_computation.1 | loop fusion | flops 16777214 | bytes 10502152 | tf_op jit(solution)/shard_map/reduce_sum | solution.py:129
  64.7 0.0 copy-start.3
  64.7 0.0 copy-done.5
  64.7 1.3 convolution_multiply_fusion
  66.0 1.6 %copy.21 = f32[2,8,64,512]{3,2,1,0:T(8,128)} copy(f32[2,8,64,512]{3,2,0,1:T(8,128)S(1)} %bitcast.44) | data formatting | bytes 4194304 | tf_op jit(solution)/shard_map/transpose | solution.py:65
  67.6 0.0 copy-done.3
  67.6 0.0 reduce-scatter.3.cloned.1.call-update
  67.6 0.0 reduce-scatter.5.cloned.1.call-start
  67.7 9.4 %reduce-scatter.3.cloned.1.call-done = f32[8,64,512]{2,1,0:T(8,128)} async-done(((f32[16,64,512]{2,1,0:T(8,128)}), f32[8,64,512]{2,1,0:T(8,128)}) %reduce-scatter.3.cloned.1.call-update) | async-done | bytes 1048592 | tf_op jit(solution)/shard_map/reduce_scatter | solution.py:66
  77.1 0.0 reduce-scatter.5.cloned.1.call-update
  77.1 4.5 %convolution_multiply_fusion.1 = f32[1024,512]{1,0:T(8,128)} fusion(bf16[1024,1024]{1,0:T(8,128)(2,1)} %copy-done.3, bf16[1024,512]{1,0:T(8,128)(2,1)} %param.7), kind=kOutput, calls=%fused_computation.15 | convolution fusion | flops 1074266112 | bytes 5242880 | tf_op jit(solution)/shard_map/dot_general | solution.py:144
  81.6 6.9 %all-to-all-start.2 = ((f32[16,64,512]{2,1,0:T(8,128)}), f32[16,64,512]{2,1,0:T(8,128)}, u32[]{:S(2)}, u32[]{:S(2)}) async-start(f32[16,64,512]{2,1,0:T(8,128)} %bitcast.43), calls=%async_computation.2 | async-start | bytes 4194304 | tf_op jit(solution)/shard_map/all_to_all | solution.py:72
  88.5 0.6 subtract_reduce_fusion.1
  91.6 18.0 %psum.28 = f32[]{:T(128)} all-reduce(f32[]{:T(128)S(6)} %add.127), channel_id=1, replica_groups=mesh['img_0'=8,'img_1'=2,'txt_0'=4,'txt_1'=4] {'img_0'}, use_global_device_ids=true, to_apply=%region_12.13 | all-reduce | flops 1 | bytes 8 | tf_op jit(solution)/shard_map/psum | solution.py:51
  109.6 3.1 %psum.29 = f32[]{:T(128)} all-reduce(f32[]{:T(128)} %psum.28), channel_id=1, replica_groups=mesh['img_0'=8,'img_1'=2,'txt_0'=4,'txt_1'=4] {'img_1'}, use_global_device_ids=true, to_apply=%region_13.14 | all-reduce | flops 1 | bytes 8 | tf_op jit(solution)/shard_map/psum | solution.py:51
  112.7 11.5 %psum.30 = f32[]{:T(128)} all-reduce(f32[]{:T(128)} %psum.29), channel_id=1, replica_groups=mesh['img_0'=8,'img_1'=2,'txt_0'=4,'txt_1'=4] {'txt_0'}, use_global_device_ids=true, to_apply=%region_14.15 | all-reduce | flops 1 | bytes 8 | tf_op jit(solution)/shard_map/psum | solution.py:51
  124.2 10.9 %psum.31 = f32[]{:T(128)} all-reduce(f32[]{:T(128)} %psum.30), channel_id=1, replica_groups=mesh['img_0'=8,'img_1'=2,'txt_0'=4,'txt_1'=4] {'txt_1'}, use_global_device_ids=true, to_apply=%region_15.16 | all-reduce | flops 1 | bytes 8 | tf_op jit(solution)/shard_map/psum | solution.py:51
  135.8 0.0 all-to-all-done.2
  135.8 2.4 %reduce_sum.89 = f32[64,512]{1,0:T(8,128)} reduce(f32[16,64,512]{2,1,0:T(8,128)} %all-to-all-done.2, f32[]{:T(128)} %constant.4.clone.1), dimensions={0}, to_apply=%region_16.17 | reduce | flops 491520 | bytes 2228228 | tf_op jit(solution)/shard_map/reduce_sum | solution.py:73
  138.2 0.0 reduce-scatter.5.cloned.1.call-done
  (68 shorter events, 1.6 us)
Async XLA Ops:
  7.2 1.7 %copy-start = (bf16[1024,1280]{1,0:T(8,128)(2,1)S(1)}, bf16[1024,1280]{1,0:T(8,128)(2,1)}, u32[]{:S(2)}) copy-start(bf16[1024,1280]{1,0:T(8,128)(2,1)} %param.4) | copy-start | bytes 7864324
  7.2 6.5 %copy-start.4 = (bf16[1024,512]{1,0:T(8,128)(2,1)S(1)}, bf16[1024,512]{1,0:T(8,128)(2,1)}, u32[]{:S(2)}) copy-start(bf16[1024,512]{1,0:T(8,128)(2,1)} %param.6) | copy-start | bytes 3145732
  8.9 4.8 %copy-start.6 = (bf16[1024,512]{1,0:T(8,128)(2,1)S(1)}, bf16[1024,512]{1,0:T(8,128)(2,1)}, u32[]{:S(2)}) copy-start(bf16[1024,512]{1,0:T(8,128)(2,1)} %param.7) | copy-start | bytes 3145732
  13.7 2.0 %copy-start.1 = (f32[1024,1024]{1,0:T(8,128)}, f32[1024,1024]{1,0:T(8,128)S(1)}, u32[]{:S(2)}) copy-start(f32[1024,1024]{1,0:T(8,128)S(1)} %get-tuple-element.50) | copy-start | bytes 12582916
  15.1 3.7 %copy-start.2 = (f32[1024,1024]{1,0:T(8,128)}, f32[1024,1024]{1,0:T(8,128)S(1)}, u32[]{:S(2)}) copy-start(f32[1024,1024]{1,0:T(8,128)S(1)} %get-tuple-element.49) | copy-start | bytes 12582916
  19.6 13.8 %all-to-all-start = ((f32[16,4,1024]{2,1,0:T(4,128)}), f32[16,4,1024]{2,1,0:T(4,128)S(1)}, u32[]{:S(2)}, u32[]{:S(2)}) async-start(f32[16,4,1024]{2,1,0:T(4,128)} %broadcast_in_dim.4), calls=%async_computation | async-start | bytes 524288 | tf_op jit(solution)/shard_map/all_to_all | solution.py:16
  34.2 19.8 %all-to-all-start.1 = ((f32[16,4,1024]{2,1,0:T(4,128)}), f32[16,4,1024]{2,1,0:T(4,128)S(1)}, u32[]{:S(2)}, u32[]{:S(2)}) async-start(f32[16,4,1024]{2,1,0:T(4,128)} %broadcast_in_dim.5), calls=%async_computation.1 | async-start | bytes 524288 | tf_op jit(solution)/shard_map/all_to_all | solution.py:16
  42.8 34.3 %reduce-scatter.3.cloned.1.call-start = ((), (), s32[]{:S(2)}) async-start(), calls=%async_computation.5 | async-start | bytes 3145728 | tf_op jit(solution)/shard_map/reduce_scatter | solution.py:66
  55.6 9.1 %copy-start.5 = (bf16[1024,512]{1,0:T(8,128)(2,1)S(1)}, bf16[1024,512]{1,0:T(8,128)(2,1)}, u32[]{:S(2)}) copy-start(bf16[1024,512]{1,0:T(8,128)(2,1)} %param.6) | copy-start | bytes 3145732
  64.7 2.9 %copy-start.3 = (bf16[1024,1024]{1,0:T(8,128)(2,1)}, bf16[1024,1024]{1,0:T(8,128)(2,1)S(1)}, u32[]{:S(2)}) copy-start(bf16[1024,1024]{1,0:T(8,128)(2,1)S(1)} %get-tuple-element.40) | copy-start | bytes 6291460
  67.6 70.6 %reduce-scatter.5.cloned.1.call-start = ((), (), s32[]{:S(2)}) async-start(), calls=%async_computation.6 | async-start | bytes 1179648 | tf_op jit(solution)/shard_map/reduce_scatter | solution.py:67
  81.6 54.2 %all-to-all-start.2 = ((f32[16,64,512]{2,1,0:T(8,128)}), f32[16,64,512]{2,1,0:T(8,128)}, u32[]{:S(2)}, u32[]{:S(2)}) async-start(f32[16,64,512]{2,1,0:T(8,128)} %bitcast.43), calls=%async_computation.2 | async-start | bytes 4194304 | tf_op jit(solution)/shard_map/all_to_all | solution.py:72
Sparse Core Ops, SparseCore 0:
  67.7 9.2 reduce-scatter.2
  80.3 39.9 reduce-scatter.4
where the time goes:
time: 147 us; the launch traced here: 146 us
  blocking collectives  43.5 us (30%)
  waiting for transfers between devices  27.8 us (19%)
  starting transfers between devices  21 us (14%)
  between operations  18.6 us (13%)
  other arithmetic  16.3 us (11%)
  matrix products  11.9 us (8%)
  local copies, waits for them, and re-layouts  7.03 us (5%)
    psum x4, blocking collectives, over_axes(): shard = lax.psum(shard, axis)  43.5 us
    all_to_all x2, waiting for transfers between devices, from_everyone(): return lax.all_to_all(copies, axis, split_axis=0, concat_axis=0, tiled=True)  18.3 us
    all_to_all x2, starting transfers between devices, from_everyone(): return lax.all_to_all(copies, axis, split_axis=0, concat_axis=0, tiled=True)  13.9 us
    reduce_scatter x1, waiting for transfers between devices, sum_by_chip(): parts = lax.psum_scatter(parts, core, scatter_dimension=0, tiled=True)  9.41 us
    reduce_sum x1, other arithmetic, body(): jnp.sum(p_col * gap) + jnp.sum(col_learn - col_teach) / img_count  9.09 us
    all_to_all x1, starting transfers between devices, summed_on_arrival(): parts = lax.all_to_all(split_up(shard, dim, size), axis, 0, 0, tiled=True)  6.9 us
    dot_general x1, matrix products, body(): jnp.einsum('id,jd->ij', teacher_img, teacher_txt, preferred_element_type=...  4.81 us
    dot_general x1, matrix products, body(): jnp.dot(picked, student_txt, preferred_element_type=jnp.float32)  4.46 us
  transfers between devices with their start and end apart: 5, of which 3 were waited for; matrix products, arithmetic and copies ran while one was open for 6% of the time, Pallas kernels for 0%

commit v1 on v0

--- a/solution.py
+++ b/solution.py
@@ -48,7 +48,8 @@
 
 def over_axes(shard, axes):
     for axis in axes:
-        shard = lax.psum(shard, axis)
+        shards = lax.all_gather(shard, axis, axis=0, tiled=False)
+        shard = shards.sum(axis=0)
     return shard
 
 

time: 147 us -> 154 us (1.048)
  local copies, waits for them, and re-layouts: 7.03 us -> 14.4 us
  other arithmetic: 16.3 us -> 18.7 us
  blocking collectives: 43.5 us -> 41.1 us
    psum x4 -> x0, blocking collectives: 43.5 us -> none  [over_axes(): shard = lax.psum(shard, axis)]
    unnamed x0 -> x4, blocking collectives: none -> 41.1 us
    unnamed x15 -> x35, local copies, waits for them, and re-layouts: 2.36 us -> 9.69 us
    reduce_sum x0 -> x4, other arithmetic: none -> 2.41 us  [over_axes(): shard = shards.sum(axis=0)]
  transfers between devices with their start and end apart: 5 -> 5, of which waited for: 3 -> 3; matrix products, arithmetic and copies ran while one was open for 6% -> 12% of each run, Pallas kernels for 0% -> 0%
where the time goes in v1:
time: 154 us
  blocking collectives  41.1 us (27%)
  waiting for transfers between devices  27.8 us (18%)
  starting transfers between devices  21.2 us (14%)
  other arithmetic  18.7 us (12%)
  between operations  18.6 us (12%)
  local copies, waits for them, and re-layouts  14.4 us (9%)
  matrix products  11.9 us (8%)
    unnamed x4, blocking collectives  41.1 us
    all_to_all x2, waiting for transfers between devices, from_everyone(): return lax.all_to_all(copies, axis, split_axis=0, concat_axis=0, tiled=True)  18.3 us
    all_to_all x2, starting transfers between devices, from_everyone(): return lax.all_to_all(copies, axis, split_axis=0, concat_axis=0, tiled=True)  13.9 us
    unnamed x35, local copies, waits for them, and re-layouts  9.69 us
    reduce_scatter x1, waiting for transfers between devices, sum_by_chip(): parts = lax.psum_scatter(parts, core, scatter_dimension=0, tiled=True)  9.41 us
    reduce_sum x1, other arithmetic, body(): jnp.sum(p_col * gap) + jnp.sum(col_learn - col_teach) / img_count  9.09 us
    all_to_all x1, starting transfers between devices, summed_on_arrival(): parts = lax.all_to_all(split_up(shard, dim, size), axis, 0, 0, tiled=True)  7.04 us
    dot_general x1, matrix products, body(): jnp.einsum('id,jd->ij', teacher_img, teacher_txt, preferred_element_type=...  4.81 us
  transfers between devices with their start and end apart: 5, of which 3 were waited for; matrix products, arithmetic and copies ran while one was open for 12% of the time, Pallas kernels for 0%

profile of v1, /device:TPU:0, one launch (start us, length us, event | category | flops | bytes accessed | tf_op | source)
XLA Modules:
  0.0 153.7 jit_solution(4704066160310405661)
XLA Ops:
  7.2 0.0 copy-start
  7.2 0.0 copy-start.4
  7.2 1.7 %copy-done = bf16[1024,1280]{1,0:T(8,128)(2,1)S(1)} copy-done((bf16[1024,1280]{1,0:T(8,128)(2,1)S(1)}, bf16[1024,1280]{1,0:T(8,128)(2,1)}, u32[]{:S(2)}) %copy-start) | copy-done | bytes 2621464
  8.9 0.0 copy-start.6
  8.9 4.8 %multiply_reduce_fusion.4 = (f32[1024]{0:T(1024)S(1)}, f32[1024]{0:T(1024)S(1)}, f32[1024,1024]{1,0:T(8,128)S(1)}) fusion(bf16[1024,1280]{1,0:T(8,128)(2,1)S(1)} %copy-done, bf16[1024,1280]{1,0:T(8,128)(2,1)} %param.5), kind=kOutput, calls=%fused_computation.12 | convolution fusion | flops 2687498240 | bytes 9445376 | tf_op jit(solution)/shard_map/id,jd->ij/dot_general | solution.py:106
  13.7 0.0 copy-done.4
  13.7 0.0 copy-done.6
  13.7 0.0 copy-start.1
  13.7 1.4 multiply_reduce_fusion.2
  15.1 0.0 copy-start.2
  15.1 0.6 copy-done.1
  15.7 1.6 %exponential_reduce_fusion.1 = (f32[1024]{0:T(1024)S(1)}, f32[1024]{0:T(1024)S(1)}) fusion(f32[1024,1024]{1,0:T(8,128)S(1)} %get-tuple-element.50, f32[1024]{0:T(1024)S(1)} %get-tuple-element.7, f32[1024]{0:T(1024)S(1)} %get-tuple-element.8), kind=kLoop, calls=%fused_computation.4 | loop fusion | flops 5240832 | bytes 4210688 | tf_op jit(solution)/shard_map/reduce_sum | solution.py:94
  17.3 1.6 %exponential_reduce_fusion = (f32[1024]{0:T(1024)S(1)}, f32[1024]{0:T(1024)S(1)}) fusion(f32[1024,1024]{1,0:T(8,128)S(1)} %get-tuple-element.49, f32[1024]{0:T(1024)S(1)} %get-tuple-element.11, f32[1024]{0:T(1024)S(1)} %get-tuple-element.12), kind=kLoop, calls=%fused_computation.3 | loop fusion | flops 5240832 | bytes 4210688 | tf_op jit(solution)/shard_map/reduce_sum | solution.py:95
  18.8 0.0 copy-done.2
  18.9 0.8 broadcast_in_dim.4
  19.6 5.3 %all-to-all-start = ((f32[16,4,1024]{2,1,0:T(4,128)}), f32[16,4,1024]{2,1,0:T(4,128)S(1)}, u32[]{:S(2)}, u32[]{:S(2)}) async-start(f32[16,4,1024]{2,1,0:T(4,128)} %broadcast_in_dim.4), calls=%async_computation | async-start | bytes 524288 | tf_op jit(solution)/shard_map/all_to_all | solution.py:16
  25.0 8.5 %all-to-all-done = f32[16,4,1024]{2,1,0:T(4,128)S(1)} async-done(((f32[16,4,1024]{2,1,0:T(4,128)}), f32[16,4,1024]{2,1,0:T(4,128)S(1)}, u32[]{:S(2)}, u32[]{:S(2)}) %all-to-all-start) | async-done | bytes 262176 | tf_op jit(solution)/shard_map/all_to_all | solution.py:16
  33.4 0.8 broadcast_in_dim.5
  34.2 8.6 %all-to-all-start.1 = ((f32[16,4,1024]{2,1,0:T(4,128)}), f32[16,4,1024]{2,1,0:T(4,128)S(1)}, u32[]{:S(2)}, u32[]{:S(2)}) async-start(f32[16,4,1024]{2,1,0:T(4,128)} %broadcast_in_dim.5), calls=%async_computation.1 | async-start | bytes 524288 | tf_op jit(solution)/shard_map/all_to_all | solution.py:16
  42.8 0.2 reduce-scatter.3.cloned.1.call-start
  43.0 0.2 fusion.8
  44.1 9.9 %all-to-all-done.1 = f32[16,4,1024]{2,1,0:T(4,128)S(1)} async-done(((f32[16,4,1024]{2,1,0:T(4,128)}), f32[16,4,1024]{2,1,0:T(4,128)S(1)}, u32[]{:S(2)}, u32[]{:S(2)}) %all-to-all-start.1) | async-done | bytes 262176 | tf_op jit(solution)/shard_map/all_to_all | solution.py:16
  54.0 0.2 fusion.9
  55.0 0.7 subtract_reduce_fusion
  55.6 0.0 copy-start.5
  55.6 9.1 %multiply_reduce_fusion = (f32[]{:T(128)}, f32[]{:T(128)}, bf16[1024,1024]{1,0:T(8,128)(2,1)S(1)}) fusion(f32[1024,1024]{1,0:T(8,128)} %copy-done.2, f32[1024,1024]{1,0:T(8,128)} %copy-done.1, f32[1024]{0:T(1024)S(1)} %bitcast.58, f32[1024]{0:T(1024)S(1)} %bitcast.55, f32[1024]{0:T(1024)S(1)} %bitcast.57, f32[1024]{0:T(1024)S(1)} %bitcast.53), kind=kLoop, calls=%fused_computation.1 | loop fusion | flops 16777214 | bytes 10502152 | tf_op jit(solution)/shard_map/reduce_sum | solution.py:130
  64.7 0.0 copy-start.3
  64.7 0.0 copy-done.5
  64.7 1.3 convolution_multiply_fusion
  66.0 1.6 %copy.21 = f32[2,8,64,512]{3,2,1,0:T(8,128)} copy(f32[2,8,64,512]{3,2,0,1:T(8,128)S(1)} %bitcast.52) | data formatting | bytes 4194304 | tf_op jit(solution)/shard_map/transpose | solution.py:66
  67.6 0.0 copy-done.3
  67.6 0.0 reduce-scatter.3.cloned.1.call-update
  67.6 0.0 reduce-scatter.5.cloned.1.call-start
  67.7 9.4 %reduce-scatter.3.cloned.1.call-done = f32[8,64,512]{2,1,0:T(8,128)} async-done(((f32[16,64,512]{2,1,0:T(8,128)}), f32[8,64,512]{2,1,0:T(8,128)}) %reduce-scatter.3.cloned.1.call-update) | async-done | bytes 1048592 | tf_op jit(solution)/shard_map/reduce_scatter | solution.py:67
  77.1 0.0 reduce-scatter.5.cloned.1.call-update
  77.1 4.5 %convolution_multiply_fusion.1 = f32[1024,512]{1,0:T(8,128)} fusion(bf16[1024,1024]{1,0:T(8,128)(2,1)} %copy-done.3, bf16[1024,512]{1,0:T(8,128)(2,1)} %param.7), kind=kOutput, calls=%fused_computation.15 | convolution fusion | flops 1074266112 | bytes 5242880 | tf_op jit(solution)/shard_map/dot_general | solution.py:145
  81.6 0.0 copy-start.10
  81.6 0.0 copy-start.9
  81.6 0.0 copy-start.8
  81.6 0.0 copy-start.7
  81.6 7.0 %all-to-all-start.2 = ((f32[16,64,512]{2,1,0:T(8,128)}), f32[16,64,512]{2,1,0:T(8,128)}, u32[]{:S(2)}, u32[]{:S(2)}) async-start(f32[16,64,512]{2,1,0:T(8,128)} %bitcast.51), calls=%async_computation.2 | async-start | bytes 4194304 | tf_op jit(solution)/shard_map/all_to_all | solution.py:73
  88.6 0.0 copy-done.10
  88.6 0.6 dynamic-slice
  89.2 0.7 subtract_reduce_fusion.1
  92.4 0.7 dynamic-update-slice
  93.2 0.0 copy-done.9
  93.2 0.6 dynamic-slice.1
  93.8 17.5 %all-reduce = f32[8]{0:T(128)S(1)} all-reduce(f32[8]{0:T(128)S(1)} %dynamic-update-slice), channel_id=1, replica_groups=mesh['img_0'=8,'img_1'=2,'txt_0'=4,'txt_1'=4] {'img_0'}, use_global_device_ids=true, to_apply=%add | all-reduce | flops 8 | bytes 64
  111.3 0.6 reduce_sum.125
  111.9 1.4 dynamic-update-slice.1
  113.3 0.0 copy-done.8
  113.3 0.6 dynamic-slice.2
  113.9 2.4 %all-reduce.1 = f32[2]{0:T(128)S(1)} all-reduce(f32[2]{0:T(128)S(1)} %dynamic-update-slice.1), channel_id=1, replica_groups=mesh['img_0'=8,'img_1'=2,'txt_0'=4,'txt_1'=4] {'img_1'}, use_global_device_ids=true, to_apply=%add.1 | all-reduce | flops 2 | bytes 16
  116.3 0.6 reduce_sum.126
  116.9 1.4 dynamic-update-slice.2
  118.4 0.0 copy-done.7
  118.4 0.6 dynamic-slice.3
  118.9 10.7 %all-reduce.2 = f32[4]{0:T(128)S(1)} all-reduce(f32[4]{0:T(128)S(1)} %dynamic-update-slice.2), channel_id=1, replica_groups=mesh['img_0'=8,'img_1'=2,'txt_0'=4,'txt_1'=4] {'txt_0'}, use_global_device_ids=true, to_apply=%add.2 | all-reduce | flops 4 | bytes 32
  129.7 0.6 reduce_sum.127
  130.3 1.4 dynamic-update-slice.3
  131.7 10.4 %all-reduce.3 = f32[4]{0:T(128)S(1)} all-reduce(f32[4]{0:T(128)S(1)} %dynamic-update-slice.3), channel_id=1, replica_groups=mesh['img_0'=8,'img_1'=2,'txt_0'=4,'txt_1'=4] {'txt_1'}, use_global_device_ids=true, to_apply=%add.3 | all-reduce | flops 4 | bytes 32
  142.0 0.6 reduce_sum.128
  143.3 0.0 all-to-all-done.2
  143.3 2.4 %reduce_sum.129 = f32[64,512]{1,0:T(8,128)} reduce(f32[16,64,512]{2,1,0:T(8,128)} %all-to-all-done.2, f32[]{:T(128)} %constant.4.clone.1), dimensions={0}, to_apply=%region_16.17 | reduce | flops 491520 | bytes 2228228 | tf_op jit(solution)/shard_map/reduce_sum | solution.py:74
  (73 shorter events, 1.6 us)
Async XLA Ops:
  7.2 1.7 %copy-start = (bf16[1024,1280]{1,0:T(8,128)(2,1)S(1)}, bf16[1024,1280]{1,0:T(8,128)(2,1)}, u32[]{:S(2)}) copy-start(bf16[1024,1280]{1,0:T(8,128)(2,1)} %param.4) | copy-start | bytes 7864324
  7.2 6.5 %copy-start.4 = (bf16[1024,512]{1,0:T(8,128)(2,1)S(1)}, bf16[1024,512]{1,0:T(8,128)(2,1)}, u32[]{:S(2)}) copy-start(bf16[1024,512]{1,0:T(8,128)(2,1)} %param.6) | copy-start | bytes 3145732
  8.9 4.8 %copy-start.6 = (bf16[1024,512]{1,0:T(8,128)(2,1)S(1)}, bf16[1024,512]{1,0:T(8,128)(2,1)}, u32[]{:S(2)}) copy-start(bf16[1024,512]{1,0:T(8,128)(2,1)} %param.7) | copy-start | bytes 3145732
  13.7 2.0 %copy-start.1 = (f32[1024,1024]{1,0:T(8,128)}, f32[1024,1024]{1,0:T(8,128)S(1)}, u32[]{:S(2)}) copy-start(f32[1024,1024]{1,0:T(8,128)S(1)} %get-tuple-element.50) | copy-start | bytes 12582916
  15.1 3.7 %copy-start.2 = (f32[1024,1024]{1,0:T(8,128)}, f32[1024,1024]{1,0:T(8,128)S(1)}, u32[]{:S(2)}) copy-start(f32[1024,1024]{1,0:T(8,128)S(1)} %get-tuple-element.49) | copy-start | bytes 12582916
  19.6 13.8 %all-to-all-start = ((f32[16,4,1024]{2,1,0:T(4,128)}), f32[16,4,1024]{2,1,0:T(4,128)S(1)}, u32[]{:S(2)}, u32[]{:S(2)}) async-start(f32[16,4,1024]{2,1,0:T(4,128)} %broadcast_in_dim.4), calls=%async_computation | async-start | bytes 524288 | tf_op jit(solution)/shard_map/all_to_all | solution.py:16
  34.2 19.8 %all-to-all-start.1 = ((f32[16,4,1024]{2,1,0:T(4,128)}), f32[16,4,1024]{2,1,0:T(4,128)S(1)}, u32[]{:S(2)}, u32[]{:S(2)}) async-start(f32[16,4,1024]{2,1,0:T(4,128)} %broadcast_in_dim.5), calls=%async_computation.1 | async-start | bytes 524288 | tf_op jit(solution)/shard_map/all_to_all | solution.py:16
  42.8 34.3 %reduce-scatter.3.cloned.1.call-start = ((), (), s32[]{:S(2)}) async-start(), calls=%async_computation.5 | async-start | bytes 3145728 | tf_op jit(solution)/shard_map/reduce_scatter | solution.py:67
  55.6 9.1 %copy-start.5 = (bf16[1024,512]{1,0:T(8,128)(2,1)S(1)}, bf16[1024,512]{1,0:T(8,128)(2,1)}, u32[]{:S(2)}) copy-start(bf16[1024,512]{1,0:T(8,128)(2,1)} %param.6) | copy-start | bytes 3145732
  64.7 2.9 %copy-start.3 = (bf16[1024,1024]{1,0:T(8,128)(2,1)}, bf16[1024,1024]{1,0:T(8,128)(2,1)S(1)}, u32[]{:S(2)}) copy-start(bf16[1024,1024]{1,0:T(8,128)(2,1)S(1)} %get-tuple-element.40) | copy-start | bytes 6291460
  67.6 78.1 %reduce-scatter.5.cloned.1.call-start = ((), (), s32[]{:S(2)}) async-start(), calls=%async_computation.6 | async-start | bytes 1179648 | tf_op jit(solution)/shard_map/reduce_scatter | solution.py:68
  81.6 7.1 %copy-start.10 = (u32[256]{0:T(256)S(1)}, u32[256]{0:T(256)}, u32[]{:S(2)}) copy-start(u32[256]{0:T(256)} %constant.24) | copy-start | bytes 3076
  81.6 11.6 %copy-start.9 = (u32[256]{0:T(256)S(1)}, u32[256]{0:T(256)}, u32[]{:S(2)}) copy-start(u32[256]{0:T(256)} %constant.29) | copy-start | bytes 3076
  81.6 31.8 %copy-start.8 = (u32[256]{0:T(256)S(1)}, u32[256]{0:T(256)}, u32[]{:S(2)}) copy-start(u32[256]{0:T(256)} %constant.34) | copy-start | bytes 3076
  81.6 36.8 %copy-start.7 = (u32[256]{0:T(256)S(1)}, u32[256]{0:T(256)}, u32[]{:S(2)}) copy-start(u32[256]{0:T(256)} %constant.39) | copy-start | bytes 3076
  81.6 61.7 %all-to-all-start.2 = ((f32[16,64,512]{2,1,0:T(8,128)}), f32[16,64,512]{2,1,0:T(8,128)}, u32[]{:S(2)}, u32[]{:S(2)}) async-start(f32[16,64,512]{2,1,0:T(8,128)} %bitcast.51), calls=%async_computation.2 | async-start | bytes 4194304 | tf_op jit(solution)/shard_map/all_to_all | solution.py:73
Sparse Core Ops, SparseCore 0:
  67.7 9.2 reduce-scatter.2
  80.3 40.1 reduce-scatter.4
